TPU v7x, 32 devices: a whole 2x2x4 slice. The times are simulated.
32 devices in a mesh: rows: 8 (over y, x, core), gz: 4 (over z).
Axes of the slice: x: 2, y: 2, z: 4, core: 2. Of those that a mesh axis runs over, the one named last changes fastest.
Arguments:
- segment_warming: float32 [64, 1024, 1024], P('gz', 'rows'), may hold values from 0.15 to 3
- eigenfunction_crosssections: float32 [10, 1024, 1024], P(None, 'rows'), may hold values from -2.5 to 2.5
- segment_phasors: float32 [64, 10], P('gz'), may hold values from 0.2 to 2
- injected_coefficients: float32 [2, 10], replicated, may hold values from -6 to 6
Outputs:
- diffused_warmth: float32 [64, 1024, 1024], P('gz', 'rows')
- refreshed_coupling_sums: float32 [64, 10, 10], P('gz')
- incoming_coefficients: float32 [64, 2, 10], P('gz')
All inputs are finite; a program needn't handle non-finite values.
Results may differ from a plain program's by a relative error of at most 0.0003.
Values sent between devices are 32-bit elements; how exact they have to be, the bound alone decides.
A program may use at most 256 MiB of HBM per device.

v0:
```python
import jax
import jax.numpy as jnp
from jax import lax
from jax.sharding import PartitionSpec as P

NX = 1024
NY = 1024
DIFFUSION_PASSES = 16


highest = lax.Precision.HIGHEST


def from_behind(block, axis, distance):
    devices = range(lax.axis_size(axis))
    route = [(i - distance, i) for i in devices if i - distance in devices]
    return lax.ppermute(block, axis, route)


def with_halo(block, sides, width):
    for axis, dim in sides:
        count = lax.axis_size(axis)
        forward = [(i, i + 1) for i in range(count - 1)]
        backward = [(target, source) for source, target in forward]
        low = lax.ppermute(
            lax.slice_in_dim(block, block.shape[dim] - width, None, axis=dim), axis, forward
        )
        high = lax.ppermute(lax.slice_in_dim(block, 0, width, axis=dim), axis, backward)
        block = jnp.concatenate([low, block, high], axis=dim)
    return block


def factor_entries(matrix):
    count = matrix.shape[-1]
    lower = [[None] * count for index in range(count)]
    for row in range(count):
        for column in range(row + 1):
            total = matrix[..., row, column]
            for inner in range(column):
                total = total - lower[row][inner] * lower[column][inner]
            if row == column:
                lower[row][column] = jnp.sqrt(total)
            else:
                lower[row][column] = total / lower[column][column]
    return lower


def cholesky_solve(lower, rhs):
    count = rhs.shape[-2]
    forward = []
    for row in range(count):
        total = rhs[..., row, :]
        for inner in range(row):
            total = total - lower[row][inner][..., None] * forward[inner]
        forward.append(total / lower[row][row][..., None])
    backward = [None] * count
    for row in range(count - 1, -1, -1):
        total = forward[row]
        for inner in range(row + 1, count):
            total = total - lower[inner][row][..., None] * backward[inner]
        backward[row] = total / lower[row][row][..., None]
    return jnp.stack(backward, axis=-2)


def propagators(constants, intersection_matrix):
    count = intersection_matrix.shape[-1]
    identity = jnp.eye(count, dtype=jnp.float32)
    doubled = intersection_matrix + jnp.swapaxes(intersection_matrix, -1, -2)
    coupled = doubled + identity * constants[..., None]
    squared = jnp.matmul(coupled, coupled, precision=highest)
    lower = factor_entries(identity + squared)
    return (cholesky_solve(lower, identity - squared), cholesky_solve(lower, 2.0 * coupled))


def rotate(matrix_real, matrix_imag, amplitude):
    real_amp = jnp.dot(matrix_real, amplitude[0], precision=highest) - jnp.dot(
        matrix_imag, amplitude[1], precision=highest
    )
    imag_amp = jnp.dot(matrix_real, amplitude[1], precision=highest) + jnp.dot(
        matrix_imag, amplitude[0], precision=highest
    )
    return jnp.stack([real_amp, imag_amp])


def complex_times(later_real, later_imag, earlier_real, earlier_imag):
    new_real = jnp.dot(later_real, earlier_real, precision=highest) - jnp.dot(
        later_imag, earlier_imag, precision=highest
    )
    new_imag = jnp.dot(later_real, earlier_imag, precision=highest) + jnp.dot(
        later_imag, earlier_real, precision=highest
    )
    return (new_real, new_imag)


def march(matrices_real, matrices_imag, amplitude):

    def advance_one(carry, pair):
        return (rotate(pair[0], pair[1], carry), carry)

    final_amp, entrances = lax.scan(advance_one, amplitude, (matrices_real, matrices_imag))
    return entrances


def pair_table(eigenfunction_crosssections):
    count = eigenfunction_crosssections.shape[0]
    flat = eigenfunction_crosssections.reshape(count, -1)
    return (flat[:, None, :] * flat[None, :, :]).reshape(count * count, -1)


def slice_coupling_sums(pairs, warmth_slices, count):
    flat_warmth = warmth_slices.reshape(warmth_slices.shape[0], -1)
    sums = lax.dot_general(flat_warmth, pairs, (((1,), (1,)), ((), ())), precision=highest)
    return (sums / float(NX * NY)).reshape(warmth_slices.shape[0], count, count)


def heat_source(eigenfunction_crosssections, amplitude):
    count = eigenfunction_crosssections.shape[0]
    flat = eigenfunction_crosssections.reshape(count, -1)
    field = jnp.einsum("zkm,mc->zkc", amplitude, flat, precision=highest)
    intensity = jnp.sum(field * field, axis=1)
    return intensity.reshape((amplitude.shape[0],) + eigenfunction_crosssections.shape[1:])


def advance(padded, source):
    side_padded = jnp.pad(padded, ((0, 0), (0, 0), (1, 1)))
    center = side_padded[:, 1:-1, 1:-1]
    laplace = (
        side_padded[:, 2:, 1:-1]
        + side_padded[:, :-2, 1:-1]
        + side_padded[:, 1:-1, 2:]
        + side_padded[:, 1:-1, :-2]
        - 4.0 * center
    )
    return center + 0.2 * laplace + 0.01 * source


def shards(segment_warming, eigenfunction_crosssections, segment_phasors, injected_coefficients):
    count = eigenfunction_crosssections.shape[0]
    pairs = pair_table(eigenfunction_crosssections)
    partial_sums = slice_coupling_sums(pairs, segment_warming, count)
    beginning_value = lax.psum(partial_sums, "rows")
    matrices_real, matrices_imag = propagators(segment_phasors, beginning_value * 0.5 * 2.0)
    identity = jnp.eye(count, dtype=jnp.float32)
    nothing = jnp.zeros_like(identity)

    def compose(carry, pair):
        return (complex_times(pair[0], pair[1], carry[0], carry[1]), None)

    products, unused = lax.scan(compose, (identity, nothing), (matrices_real, matrices_imag))
    product_real, product_imag = products
    position = lax.axis_index("gz")
    entrance = injected_coefficients
    for section in range(lax.axis_size("gz") - 1):
        passed = from_behind(rotate(product_real, product_imag, entrance), "gz", 1)
        entrance = jnp.where(position == section + 1, passed, entrance)
    incoming_coefficients = march(matrices_real, matrices_imag, entrance)
    source = heat_source(eigenfunction_crosssections, incoming_coefficients)
    rows_here = segment_warming.shape[1]
    margin = 4
    widened_source = with_halo(source, (("rows", 1),), margin)
    global_rows = lax.axis_index("rows") * rows_here - margin + jnp.arange(rows_here + 2 * margin)
    inside = ((global_rows >= 0) & (global_rows < NX)).astype(jnp.float32)[None, :, None]
    inner_source = widened_source[:, 1:-1]
    diffused_warmth = segment_warming
    for block in range(DIFFUSION_PASSES // margin):
        widened = with_halo(diffused_warmth, (("rows", 1),), margin)
        for subcycle in range(margin):
            inner = advance(widened, inner_source)
            widened = jnp.pad(inner, ((0, 0), (1, 1), (0, 0))) * inside
        diffused_warmth = widened[:, margin:-margin]
    final_sums = slice_coupling_sums(pairs, diffused_warmth, count)
    refreshed_coupling_sums = lax.psum(final_sums, "rows")
    return (diffused_warmth, refreshed_coupling_sums, incoming_coefficients)


def solution(mesh):
    placed = (P("gz", "rows", None), P(None, "rows", None), P("gz", None), P())
    return jax.shard_map(
        shards,
        mesh=mesh,
        in_specs=placed,
        out_specs=(P("gz", "rows", None), P("gz", None, None), P("gz", None, None)),
        check_vma=False,
    )
```

profile of v0, /device:TPU:20, one launch (start us, length us, event | category | flops | bytes accessed | tf_op | source)
XLA Modules:
  0.0 678.7 jit_solution(1253212601768647431)
XLA Ops:
  4.1 8.3 %copy.35 = f32[2,8,128,1024]{3,1,2,0:T(8,128)} copy(f32[2,8,128,1024]{3,2,1,0:T(8,128)S(1)} %bitcast.805) | data formatting | bytes 16777216
  12.3 53.0 %broadcast_multiply_fusion = f32[10,10,131072]{2,1,0:T(8,128)} fusion(f32[10,131072]{1,0:T(8,128)} %bitcast.799), kind=kLoop, calls=%fused_computation.55 | loop fusion | flops 13107200 | bytes 57671680 | tf_op jit(solution)/shard_map/mul | solution.py:107
  65.3 62.7 %mul.8205 = f32[100,131072]{1,0:T(8,128)} reshape(f32[10,10,131072]{2,1,0:T(8,128)} %broadcast_multiply_fusion) | data formatting | bytes 104857600 | tf_op jit(solution)/shard_map/mul | solution.py:107
  128.1 8.2 %copy.36 = f32[2,8,128,1024]{3,1,2,0:T(8,128)S(1)} copy(f32[2,8,128,1024]{3,2,1,0:T(8,128)} %bitcast.801) | data formatting | bytes 16777216
  136.3 47.6 %fusion.144 = f32[16,100]{1,0:T(8,128)S(1)} fusion(f32[100,131072]{1,0:T(8,128)} %mul.8205, f32[16,131072]{1,0:T(8,128)S(1)} %bitcast.802), kind=kOutput, calls=%fused_computation.225 | convolution fusion | flops 2516583936 | bytes 60823808 | tf_op jit(solution)/shard_map/dot_general | solution.py:112
  184.1 24.0 %psum.14 = f32[16,10,10]{0,2,1:T(8,128)S(1)} all-reduce(f32[16,10,10]{0,2,1:T(8,128)S(1)} %reshape.12489), channel_id=1, replica_groups=mesh['rows'=8,'gz'=4] {'rows'}, use_global_device_ids=true, to_apply=%region_0.0 | all-reduce | flops 1600 | bytes 12800 | tf_op jit(solution)/shard_map/psum | solution.py:141
  211.0 9.2 %while.26 = (s32[]{:T(128)}, f32[10,10]{1,0:T(8,128)S(1)}, f32[10,10]{1,0:T(8,128)S(1)}, f32[16,10,10]{2,1,0:T(8,128)S(1)}, f32[16,10,10]{2,1,0:T(8,128)S(1)}, /*index=5*/s32[]{:T(128)}, s32[]{:T(128)}) while((s32[]{:T(128)}, f32[10,10]{1,0:T(8,128)S(1)}, f32[10,10]{1,0:T(8,128)S(1)}, f32[16,10,10]{2,1,0:T(8,128)S(1)}, ...), condition=%wide.region_2.3_spmd.clone, body=%wide.region_1.2_spmd.clone.sunk | while | flops 48403 | bytes 84424 | solution.py:149
  227.5 4.5 collective-permute-start.1
  232.0 6.3 reshape.12525
  250.5 9.8 %while.25 = (s32[]{:T(128)}, f32[2,10]{1,0:T(2,128)S(1)}, f32[16,2,10]{2,1,0:T(2,128)S(1)}, f32[16,10,10]{2,1,0:T(8,128)S(1)}, f32[16,10,10]{2,1,0:T(8,128)S(1)}, /*index=5*/s32[]{:T(128)}) while((s32[]{:T(128)}, f32[2,10]{1,0:T(2,128)S(1)}, f32[16,2,10]{2,1,0:T(2,128)S(1)}, f32[16,10,10]{2,1,0:T(8,128)S(1)}, f32[16,10,10]{2,1,0:T(8,128)S(1)}, ...), condition=%wide.region_4.5_spmd, body=%wide.region_3.4_spmd.sunk | while | flops 4842 | bytes 38297 | solution.py:100
  260.3 20.5 %fusion.143 = f32[16,131072]{1,0:T(8,128)S(1)} fusion(f32[10,131072,1]{1,0,2:T(8,128)} %reshape.12525, f32[16,2,10]{2,1,0:T(2,128)S(1)} %get-tuple-element.97), kind=kOutput, calls=%fused_computation.223 | convolution fusion | flops 509607936 | bytes 13632768 | tf_op jit(solution)/shard_map/zkm,mc->zkc/dot_general | solution.py:119
  280.8 4.9 copy.37
  297.4 10.3 %fusion.51 = f32[16,134,1024]{2,1,0:T(8,128)} fusion(f32[16,136,1024]{2,1,0:T(8,128)S(1)} %pad_maximum_fusion.3, f32[16,4,1024]{2,1,0:T(4,128)S(1)} %collective-permute-done.6, f32[16,128,1024]{2,1,0:T(8,128)S(1)} %bitcast.781, f32[16,4,1024]{2,1,0:T(4,128)S(1)} %collective-permute-done.5), kind=kLoop, calls=%fused_computation.93 | loop fusion | flops 24150016 | bytes 53346304 | tf_op jit(solution)/shard_map/add | solution.py:134
  307.8 4.8 pad_multiply_fusion.14
  312.6 10.4 %fusion.57 = f32[16,134,1024]{2,1,0:T(8,128)} fusion(f32[16,136,1024]{2,1,0:T(8,128)S(1)} %pad_multiply_fusion.14, f32[16,4,1024]{2,1,0:T(4,128)S(1)} %collective-permute-done.6, f32[16,128,1024]{2,1,0:T(8,128)S(1)} %bitcast.782, f32[16,4,1024]{2,1,0:T(4,128)S(1)} %collective-permute-done.5), kind=kLoop, calls=%fused_computation.99 | loop fusion | flops 24150016 | bytes 53346304 | tf_op jit(solution)/shard_map/add | solution.py:134
  323.0 4.8 pad_multiply_fusion.13
  327.9 10.4 %fusion.63 = f32[16,134,1024]{2,1,0:T(8,128)} fusion(f32[16,136,1024]{2,1,0:T(8,128)S(1)} %pad_multiply_fusion.13, f32[16,4,1024]{2,1,0:T(4,128)S(1)} %collective-permute-done.6, f32[16,128,1024]{2,1,0:T(8,128)S(1)} %bitcast.783, f32[16,4,1024]{2,1,0:T(4,128)S(1)} %collective-permute-done.5), kind=kLoop, calls=%fused_computation.105 | loop fusion | flops 24150016 | bytes 53346304 | tf_op jit(solution)/shard_map/add | solution.py:134
  338.2 4.8 pad_multiply_fusion.12
  343.1 10.5 %fusion.69 = f32[16,134,1024]{2,1,0:T(8,128)} fusion(f32[16,136,1024]{2,1,0:T(8,128)S(1)} %pad_multiply_fusion.12, f32[16,4,1024]{2,1,0:T(4,128)S(1)} %collective-permute-done.6, f32[16,128,1024]{2,1,0:T(8,128)S(1)} %bitcast.784, f32[16,4,1024]{2,1,0:T(4,128)S(1)} %collective-permute-done.5), kind=kLoop, calls=%fused_computation.111 | loop fusion | flops 24150016 | bytes 53346304 | tf_op jit(solution)/shard_map/add | solution.py:134
  353.6 4.8 pad_multiply_fusion.11
  373.7 10.4 %fusion.75 = f32[16,134,1024]{2,1,0:T(8,128)} fusion(f32[16,136,1024]{2,1,0:T(8,128)S(1)} %pad_maximum_fusion.4, f32[16,4,1024]{2,1,0:T(4,128)S(1)} %collective-permute-done.6, f32[16,128,1024]{2,1,0:T(8,128)S(1)} %bitcast.785, f32[16,4,1024]{2,1,0:T(4,128)S(1)} %collective-permute-done.5), kind=kLoop, calls=%fused_computation.117 | loop fusion | flops 24150016 | bytes 53346304 | tf_op jit(solution)/shard_map/add | solution.py:134
  384.0 4.8 pad_multiply_fusion.10
  388.9 10.4 %fusion.81 = f32[16,134,1024]{2,1,0:T(8,128)} fusion(f32[16,136,1024]{2,1,0:T(8,128)S(1)} %pad_multiply_fusion.10, f32[16,4,1024]{2,1,0:T(4,128)S(1)} %collective-permute-done.6, f32[16,128,1024]{2,1,0:T(8,128)S(1)} %bitcast.786, f32[16,4,1024]{2,1,0:T(4,128)S(1)} %collective-permute-done.5), kind=kLoop, calls=%fused_computation.123 | loop fusion | flops 24150016 | bytes 53346304 | tf_op jit(solution)/shard_map/add | solution.py:134
  399.2 4.8 pad_multiply_fusion.9
  404.1 10.4 %fusion.87 = f32[16,134,1024]{2,1,0:T(8,128)} fusion(f32[16,136,1024]{2,1,0:T(8,128)S(1)} %pad_multiply_fusion.9, f32[16,4,1024]{2,1,0:T(4,128)S(1)} %collective-permute-done.6, f32[16,128,1024]{2,1,0:T(8,128)S(1)} %bitcast.787, f32[16,4,1024]{2,1,0:T(4,128)S(1)} %collective-permute-done.5), kind=kLoop, calls=%fused_computation.129 | loop fusion | flops 24150016 | bytes 53346304 | tf_op jit(solution)/shard_map/add | solution.py:134
  414.5 4.8 pad_multiply_fusion.8
  419.3 10.8 %fusion.93 = f32[16,134,1024]{2,1,0:T(8,128)} fusion(f32[16,136,1024]{2,1,0:T(8,128)S(1)} %pad_multiply_fusion.8, f32[16,4,1024]{2,1,0:T(4,128)S(1)} %collective-permute-done.6, f32[16,128,1024]{2,1,0:T(8,128)S(1)} %bitcast.788, f32[16,4,1024]{2,1,0:T(4,128)S(1)} %collective-permute-done.5), kind=kLoop, calls=%fused_computation.135 | loop fusion | flops 24150016 | bytes 53346304 | tf_op jit(solution)/shard_map/add | solution.py:134
  430.1 4.8 pad_multiply_fusion.7
  451.9 10.4 %fusion.99 = f32[16,134,1024]{2,1,0:T(8,128)} fusion(f32[16,136,1024]{2,1,0:T(8,128)S(1)} %pad_maximum_fusion.5, f32[16,4,1024]{2,1,0:T(4,128)S(1)} %collective-permute-done.6, f32[16,128,1024]{2,1,0:T(8,128)S(1)} %bitcast.789, f32[16,4,1024]{2,1,0:T(4,128)S(1)} %collective-permute-done.5), kind=kLoop, calls=%fused_computation.141 | loop fusion | flops 24150016 | bytes 53346304 | tf_op jit(solution)/shard_map/add | solution.py:134
  462.2 4.8 pad_multiply_fusion.6
  467.1 10.4 %fusion.105 = f32[16,134,1024]{2,1,0:T(8,128)} fusion(f32[16,136,1024]{2,1,0:T(8,128)S(1)} %pad_multiply_fusion.6, f32[16,4,1024]{2,1,0:T(4,128)S(1)} %collective-permute-done.6, f32[16,128,1024]{2,1,0:T(8,128)S(1)} %bitcast.790, f32[16,4,1024]{2,1,0:T(4,128)S(1)} %collective-permute-done.5), kind=kLoop, calls=%fused_computation.147 | loop fusion | flops 24150016 | bytes 53346304 | tf_op jit(solution)/shard_map/add | solution.py:134
  477.4 4.8 pad_multiply_fusion.5
  482.3 10.4 %fusion.111 = f32[16,134,1024]{2,1,0:T(8,128)} fusion(f32[16,136,1024]{2,1,0:T(8,128)S(1)} %pad_multiply_fusion.5, f32[16,4,1024]{2,1,0:T(4,128)S(1)} %collective-permute-done.6, f32[16,128,1024]{2,1,0:T(8,128)S(1)} %bitcast.791, f32[16,4,1024]{2,1,0:T(4,128)S(1)} %collective-permute-done.5), kind=kLoop, calls=%fused_computation.153 | loop fusion | flops 24150016 | bytes 53346304 | tf_op jit(solution)/shard_map/add | solution.py:134
  492.7 4.8 pad_multiply_fusion.4
  497.5 10.5 %fusion.117 = f32[16,134,1024]{2,1,0:T(8,128)} fusion(f32[16,136,1024]{2,1,0:T(8,128)S(1)} %pad_multiply_fusion.4, f32[16,4,1024]{2,1,0:T(4,128)S(1)} %collective-permute-done.6, f32[16,128,1024]{2,1,0:T(8,128)S(1)} %bitcast.792, f32[16,4,1024]{2,1,0:T(4,128)S(1)} %collective-permute-done.5), kind=kLoop, calls=%fused_computation.159 | loop fusion | flops 24150016 | bytes 53346304 | tf_op jit(solution)/shard_map/add | solution.py:134
  508.1 4.9 pad_multiply_fusion.3
  523.8 9.1 %slice.892 = f32[16,128,1024]{2,1,0:T(8,128)} slice(f32[16,136,1024]{2,1,0:T(8,128)} %copy-done.1), slice={[0:16], [4:132], [0:1024]} | slice | bytes 16777216 | tf_op jit(solution)/shard_map/slice | solution.py:170
  537.5 10.3 %fusion.123 = f32[16,134,1024]{2,1,0:T(8,128)} fusion(f32[16,136,1024]{2,1,0:T(8,128)S(1)} %pad_maximum_fusion.6, f32[16,4,1024]{2,1,0:T(4,128)S(1)} %collective-permute-done.6, f32[16,128,1024]{2,1,0:T(8,128)S(1)} %bitcast.795, f32[16,4,1024]{2,1,0:T(4,128)S(1)} %collective-permute-done.5), kind=kLoop, calls=%fused_computation.165 | loop fusion | flops 24150016 | bytes 53346304 | tf_op jit(solution)/shard_map/add | solution.py:134
  547.9 4.8 pad_multiply_fusion.2
  552.7 10.4 %fusion.129 = f32[16,134,1024]{2,1,0:T(8,128)} fusion(f32[16,136,1024]{2,1,0:T(8,128)S(1)} %pad_multiply_fusion.2, f32[16,4,1024]{2,1,0:T(4,128)S(1)} %collective-permute-done.6, f32[16,128,1024]{2,1,0:T(8,128)S(1)} %bitcast.796, f32[16,4,1024]{2,1,0:T(4,128)S(1)} %collective-permute-done.5), kind=kLoop, calls=%fused_computation.171 | loop fusion | flops 24150016 | bytes 53346304 | tf_op jit(solution)/shard_map/add | solution.py:134
  563.1 4.8 pad_multiply_fusion.1
  567.9 10.4 %fusion.135 = f32[16,134,1024]{2,1,0:T(8,128)} fusion(f32[16,136,1024]{2,1,0:T(8,128)S(1)} %pad_multiply_fusion.1, f32[16,4,1024]{2,1,0:T(4,128)S(1)} %collective-permute-done.6, f32[16,128,1024]{2,1,0:T(8,128)S(1)} %bitcast.797, f32[16,4,1024]{2,1,0:T(4,128)S(1)} %collective-permute-done.5), kind=kLoop, calls=%fused_computation.177 | loop fusion | flops 24150016 | bytes 53346304 | tf_op jit(solution)/shard_map/add | solution.py:134
  578.3 4.8 pad_multiply_fusion
  583.2 10.6 %fusion.141 = f32[16,134,1024]{2,1,0:T(8,128)} fusion(f32[16,136,1024]{2,1,0:T(8,128)S(1)} %pad_multiply_fusion, f32[16,4,1024]{2,1,0:T(4,128)S(1)} %collective-permute-done.6, f32[16,128,1024]{2,1,0:T(8,128)S(1)} %bitcast.798, f32[16,4,1024]{2,1,0:T(4,128)S(1)} %collective-permute-done.5), kind=kLoop, calls=%fused_computation.183 | loop fusion | flops 24150016 | bytes 53346304 | tf_op jit(solution)/shard_map/add | solution.py:134
  593.7 4.8 pad_multiply_fusion.15
  601.9 4.9 copy.38
  606.8 47.5 %convolution_multiply_fusion.2 = f32[16,100]{1,0:T(8,128)S(1)} fusion(f32[16,131072]{1,0:T(8,128)S(1)} %bitcast.800, f32[100,131072]{1,0:T(8,128)} %mul.8205), kind=kOutput, calls=%fused_computation.226 | convolution fusion | flops 2516583936 | bytes 60823808 | tf_op jit(solution)/shard_map/dot_general | solution.py:112
  654.4 23.1 %psum.15 = f32[16,10,10]{0,2,1:T(8,128)S(1)} all-reduce(f32[16,10,10]{0,2,1:T(8,128)S(1)} %reshape.12492), channel_id=1, replica_groups=mesh['rows'=8,'gz'=4] {'rows'}, use_global_device_ids=true, to_apply=%region_6.7 | all-reduce | flops 1600 | bytes 12800 | tf_op jit(solution)/shard_map/psum | solution.py:172
  (292 shorter events, 107.5 us)
Async XLA Ops:
  136.3 71.8 %copy-start.6 = (f32[16,10]{1,0:T(8,128)S(1)}, f32[16,10]{1,0:T(8,128)}, u32[]{:S(2)}) copy-start(f32[16,10]{1,0:T(8,128)} %param.10) | copy-start | bytes 1924
  136.3 83.9 %copy-start.5 = (f32[2,10]{1,0:T(2,128)S(1)}, f32[2,10]{1,0:T(2,128)}, u32[]{:S(2)}) copy-start(f32[2,10]{1,0:T(2,128)} %param.11) | copy-start | bytes 244
  220.7 17.6 %collective-permute-start.2 = (f32[2,10]{1,0:T(2,128)S(1)}, f32[2,10]{1,0:T(2,128)S(1)}, u32[]{:S(2)}, u32[]{:S(2)}) collective-permute-start(f32[2,10]{1,0:T(2,128)S(1)} %pad_maximum_fusion.7), channel_id=1, source_target_pairs={{0,1},{1,2},{2,3},{4,5},{5,6},{6,7},{8,9},{9,10},{10,11},{12,13},{... | collective-permute-start | bytes 248 | tf_op jit(solution)/shard_map/ppermute | solution.py:17
  225.6 67.1 %collective-permute-start = (f32[16,4,1024]{2,1,0:T(4,128)S(1)}, f32[16,4,1024]{2,1,0:T(4,128)S(1)}, u32[]{:S(2)}, u32[]{:S(2)}) collective-permute-start(f32[16,4,1024]{2,1,0:T(4,128)S(1)} %get-tuple-element.274), channel_id=1, source_target_pairs={{0,4},{4,8},{8,12},{12,16},{16,20},{20,24},{24,28},{1,5},{5,9},{9,... | collective-permute-start | bytes 786440 | tf_op jit(solution)/shard_map/ppermute | solution.py:25
  227.5 65.2 %collective-permute-start.1 = (f32[16,4,1024]{2,1,0:T(4,128)S(1)}, f32[16,4,1024]{2,1,0:T(4,128)S(1)}, u32[]{:S(2)}, u32[]{:S(2)}) collective-permute-start(f32[16,4,1024]{2,1,0:T(4,128)S(1)} %get-tuple-element.275), channel_id=1, source_target_pairs={{4,0},{8,4},{12,8},{16,12},{20,16},{24,20},{28,24},{5,1},{9,5},{13... | collective-permute-start | bytes 786440 | tf_op jit(solution)/shard_map/ppermute | solution.py:28
  239.0 5.5 collective-permute-start.3
  245.0 5.5 collective-permute-start.4
  260.3 25.4 %copy-start.3 = (f32[16,2,10]{2,1,0:T(2,128)}, f32[16,2,10]{2,1,0:T(2,128)S(1)}, u32[]{:S(2)}) copy-start(f32[16,2,10]{2,1,0:T(2,128)S(1)} %get-tuple-element.97) | copy-start | bytes 3844
  285.7 211.8 %copy-start = (f32[2,8,128,1024]{3,2,1,0:T(8,128)}, f32[2,8,128,1024]{3,2,1,0:T(8,128)S(1)}, u32[]{:S(2)}) copy-start(f32[2,8,128,1024]{3,2,1,0:T(8,128)S(1)} %copy.37) | copy-start | bytes 25165828
  285.8 11.6 %collective-permute-start.5 = (f32[16,4,1024]{2,1,0:T(4,128)S(1)}, f32[16,4,1024]{2,1,0:T(4,128)S(1)}, u32[]{:S(2)}, u32[]{:S(2)}) collective-permute-start(f32[16,4,1024]{2,1,0:T(4,128)S(1)} %get-tuple-element.272), channel_id=1, source_target_pairs={{0,4},{4,8},{8,12},{12,16},{16,20},{20,24},{24,28},{1,5},{5,9},{9,... | collective-permute-start | bytes 786440 | tf_op jit(solution)/shard_map/ppermute | solution.py:25
  288.1 9.3 %collective-permute-start.6 = (f32[16,4,1024]{2,1,0:T(4,128)S(1)}, f32[16,4,1024]{2,1,0:T(4,128)S(1)}, u32[]{:S(2)}, u32[]{:S(2)}) collective-permute-start(f32[16,4,1024]{2,1,0:T(4,128)S(1)} %get-tuple-element.273), channel_id=1, source_target_pairs={{4,0},{8,4},{12,8},{16,12},{20,16},{24,20},{28,24},{5,1},{9,5},{13... | collective-permute-start | bytes 786440 | tf_op jit(solution)/shard_map/ppermute | solution.py:28
  358.6 10.9 %collective-permute-start.7 = (f32[16,4,1024]{2,1,0:T(4,128)S(1)}, f32[16,4,1024]{2,1,0:T(4,128)S(1)}, u32[]{:S(2)}, u32[]{:S(2)}) collective-permute-start(f32[16,4,1024]{2,1,0:T(4,128)S(1)} %get-tuple-element.270), channel_id=1, source_target_pairs={{0,4},{4,8},{8,12},{12,16},{16,20},{20,24},{24,28},{1,5},{5,9},{9,... | collective-permute-start | bytes 786440 | tf_op jit(solution)/shard_map/ppermute | solution.py:25
  360.5 9.0 %collective-permute-start.8 = (f32[16,4,1024]{2,1,0:T(4,128)S(1)}, f32[16,4,1024]{2,1,0:T(4,128)S(1)}, u32[]{:S(2)}, u32[]{:S(2)}) collective-permute-start(f32[16,4,1024]{2,1,0:T(4,128)S(1)} %get-tuple-element.271), channel_id=1, source_target_pairs={{4,0},{8,4},{12,8},{16,12},{20,16},{24,20},{28,24},{5,1},{9,5},{13... | collective-permute-start | bytes 786440 | tf_op jit(solution)/shard_map/ppermute | solution.py:28
  435.0 10.5 %collective-permute-start.10 = (f32[16,4,1024]{2,1,0:T(4,128)S(1)}, f32[16,4,1024]{2,1,0:T(4,128)S(1)}, u32[]{:S(2)}, u32[]{:S(2)}) collective-permute-start(f32[16,4,1024]{2,1,0:T(4,128)S(1)} %get-tuple-element.269), channel_id=1, source_target_pairs={{4,0},{8,4},{12,8},{16,12},{20,16},{24,20},{28,24},{5,1},{9,5},{13... | collective-permute-start | bytes 786440 | tf_op jit(solution)/shard_map/ppermute | solution.py:28
  439.2 8.6 %collective-permute-start.9 = (f32[16,4,1024]{2,1,0:T(4,128)S(1)}, f32[16,4,1024]{2,1,0:T(4,128)S(1)}, u32[]{:S(2)}, u32[]{:S(2)}) collective-permute-start(f32[16,4,1024]{2,1,0:T(4,128)S(1)} %get-tuple-element.268), channel_id=1, source_target_pairs={{0,4},{4,8},{8,12},{12,16},{16,20},{20,24},{24,28},{1,5},{5,9},{9,... | collective-permute-start | bytes 786440 | tf_op jit(solution)/shard_map/ppermute | solution.py:25
  508.1 15.0 %copy-start.4 = (f32[16,2,10]{2,1,0:T(2,128)S(1)}, f32[16,2,10]{2,1,0:T(2,128)}, u32[]{:S(2)}) copy-start(f32[16,2,10]{2,1,0:T(2,128)} %copy-done.3) | copy-start | bytes 3844
  512.9 3.5 copy-start.1
  516.5 16.4 %collective-permute-start.11 = (f32[16,4,1024]{2,1,0:T(4,128)S(1)}, f32[16,4,1024]{2,1,0:T(4,128)S(1)}, u32[]{:S(2)}, u32[]{:S(2)}) collective-permute-start(f32[16,4,1024]{2,1,0:T(4,128)S(1)} %get-tuple-element.266), channel_id=1, source_target_pairs={{0,4},{4,8},{8,12},{12,16},{16,20},{20,24},{24,28},{1,5},{5,9},{9,... | collective-permute-start | bytes 786440 | tf_op jit(solution)/shard_map/ppermute | solution.py:25
  518.5 14.4 %collective-permute-start.12 = (f32[16,4,1024]{2,1,0:T(4,128)S(1)}, f32[16,4,1024]{2,1,0:T(4,128)S(1)}, u32[]{:S(2)}, u32[]{:S(2)}) collective-permute-start(f32[16,4,1024]{2,1,0:T(4,128)S(1)} %get-tuple-element.267), channel_id=1, source_target_pairs={{4,0},{8,4},{12,8},{16,12},{20,16},{24,20},{28,24},{5,1},{9,5},{13... | collective-permute-start | bytes 786440 | tf_op jit(solution)/shard_map/ppermute | solution.py:28
  523.8 13.4 %slice-start = ((s8[8388608]{0:T(1024)(128)(4,1)}), s8[4194304]{0:T(1024)(128)(4,1)S(1)}, s32[]{:S(2)}) async-start(s8[8388608]{0:T(1024)(128)(4,1)} %bitcast.793), calls=%async_computation | async-start | bytes 8388608
  532.9 4.6 slice-start.1
  598.5 3.4 copy-start.2
where the time goes:
time: 684 us; the launch traced here: 679 us
  other arithmetic  316 us (46%)
  matrix products  135 us (20%)
  local copies, waits for them, and re-layouts  129 us (19%)
  blocking collectives  47.1 us (7%)
  starting transfers between devices  39.6 us (6%)
  waiting for transfers between devices  9.87 us (1%)
    add x16, other arithmetic, advance(): return center + 0.2 * laplace + 0.01 * source  167 us
    dot_general x2, matrix products, slice_coupling_sums(): lax.dot_general(flat_warmth, pairs, (((1,), (1,)), ((), ())), precision=h...  95.1 us
    mul x16, other arithmetic, shards(): widened = jnp.pad(inner, ((0, 0), (1, 1), (0, 0))) * inside  77.4 us
    mul x2, local copies, waits for them, and re-layouts, pair_table(): return (flat[:, None, :] * flat[None, :, :]).reshape(count * count, -1)  69.1 us
    mul x1, other arithmetic, pair_table(): return (flat[:, None, :] * flat[None, :, :]).reshape(count * count, -1)  53 us
    unnamed x28, local copies, waits for them, and re-layouts  38.7 us
    psum x1, blocking collectives, shards(): beginning_value = lax.psum(partial_sums, 'rows')  24 us
    psum x1, blocking collectives, shards(): refreshed_coupling_sums = lax.psum(final_sums, 'rows')  23.1 us
  transfers between devices with their start and end apart: 13, of which 4 were waited for; matrix products, arithmetic and copies ran while one was open for 10% of the time, Pallas kernels for 0%

commit v1 on v0

v1 whole, which is shorter than its diff:
```python
import functools
import math

import jax
import jax.numpy as jnp
import numpy as np
from jax import lax
from jax.experimental import pallas as pl
from jax.experimental.pallas import tpu as pltpu
from jax.sharding import PartitionSpec as P

PASSES = 16
LANES = 128
SUB = 8
MIB = 1024 * 1024
MESH = pl.DeviceIdType.MESH
highest = lax.Precision.HIGHEST


def pair_list(count):
    return [(m, n) for m in range(count) for n in range(m, count)]


def padded(size, unit):
    return -(-size // unit) * unit


def iota(shape, dim):
    return lax.broadcasted_iota(jnp.int32, shape, dim)


def split(value):
    high = value.astype(jnp.bfloat16)
    low = (value - high.astype(jnp.float32)).astype(jnp.bfloat16)
    return high, low


def write_pairs(count, modes, pairs_ref):
    pairs = pair_list(count)
    half = pairs_ref.shape[0] // 2
    for first in range(0, half // SUB, 2):
        products = []
        for pair in range(first, first + 2):
            if pair < len(pairs):
                m, n = pairs[pair]
                products.append(modes(m) * modes(n))
            else:
                products.append(jnp.zeros_like(products[0]))
        high, low = split(jnp.concatenate(products, axis=0))
        at = first * SUB
        pairs_ref[at : at + 2 * SUB] = high
        pairs_ref[half + at : half + at + 2 * SUB] = low


def gram_step(warmth, pairs_ref, warm_ref, total):
    slots = warmth.shape[0]
    high, low = split(warmth)
    warm_ref[:slots] = high
    warm_ref[slots:] = low
    total[...] += lax.dot_general(
        pairs_ref[...],
        warm_ref[...],
        (((1,), (1,)), ((), ())),
        preferred_element_type=jnp.float32,
    )


def gram_finish(total, slices, row_major):
    half = total.shape[0] // 2
    slots = total.shape[1] // 2
    both = (total[half:, slots:] + total[half:, :slots]) + total[:half, slots:] + total[:half, :slots]
    row = iota((half, slots), 0) % SUB
    column = iota((half, slots), 1)
    column_row = column // slices if row_major else column % SUB
    kept = jnp.where(row == column_row, both, 0.0)
    kept = jnp.sum(kept.reshape(half // SUB, SUB, slots), axis=1)
    source = iota((slots, LANES), 0)
    source_slice = source % slices if row_major else source // SUB
    gather = (source_slice == iota((slots, LANES), 1)).astype(jnp.float32)
    return jnp.dot(kept, gather, precision=highest, preferred_element_type=jnp.float32)


def gram_kernel(warm_ref, mode_ref, out_ref, pairs_ref, split_ref, total):
    count = mode_ref.shape[0]
    slices = warm_ref.shape[0]

    @pl.when(pl.program_id(0) == 0)
    def _():
        total[...] = jnp.zeros_like(total)

    write_pairs(count, lambda m: mode_ref[m], pairs_ref)
    gram_step(warm_ref[...].reshape(slices * SUB, warm_ref.shape[2]), pairs_ref, split_ref, total)

    @pl.when(pl.program_id(0) == pl.num_programs(0) - 1)
    def _():
        out_ref[...] = gram_finish(total[...], slices, False)


def gram(warm, modes):
    slices, rows, width = warm.shape
    count = modes.shape[0]
    pair_rows = padded(len(pair_list(count)), 2) * SUB
    return pl.pallas_call(
        gram_kernel,
        grid=(rows // SUB,),
        out_shape=jax.ShapeDtypeStruct((pair_rows // SUB, LANES), jnp.float32),
        in_specs=[
            pl.BlockSpec((slices, SUB, width), lambda i: (0, i, 0)),
            pl.BlockSpec((count, SUB, width), lambda i: (0, i, 0)),
        ],
        out_specs=pl.BlockSpec((pair_rows // SUB, LANES), lambda i: (0, 0)),
        scratch_shapes=[
            pltpu.VMEM((2 * pair_rows, width), jnp.bfloat16),
            pltpu.VMEM((2 * slices * SUB, width), jnp.bfloat16),
            pltpu.VMEM((2 * pair_rows, 2 * slices * SUB), jnp.float32),
        ],
        compiler_params=pltpu.CompilerParams(vmem_limit_bytes=40 * MIB),
        cost_estimate=pl.CostEstimate(flops=20_000_000_000, bytes_accessed=14_000_000, transcendentals=0),
    )(warm, modes)


def share_rows(part_ref, gathered, send_sem, recv_sem, nr):
    me = lax.axis_index("rows")
    copies = []
    for d in range(1, nr):
        copy = pltpu.make_async_remote_copy(
            src_ref=part_ref,
            dst_ref=gathered.at[me],
            send_sem=send_sem.at[d],
            recv_sem=recv_sem.at[d],
            device_id={"rows": lax.rem(me + d, nr)},
            device_id_type=MESH,
        )
        copy.start()
        copies.append(copy)
    gathered[me] = part_ref[...]
    for copy in copies:
        copy.wait()
    total = gathered[0]
    for r in range(1, nr):
        total = total + gathered[r]
    return total


def meet(nr, ng):
    barrier = pltpu.get_barrier_semaphore()
    me = lax.axis_index("rows")
    for d in range(1, nr):
        pl.semaphore_signal(barrier, inc=1, device_id={"rows": lax.rem(me + d, nr)}, device_id_type=MESH)
    gz = lax.axis_index("gz")
    for d in range(1, ng):
        pl.semaphore_signal(barrier, inc=1, device_id={"gz": lax.rem(gz + d, ng)}, device_id_type=MESH)
    pl.semaphore_wait(barrier, nr - 1 + ng - 1)


def spread(row, rows):
    return jnp.broadcast_to(row, (rows, row.shape[1]))


def propagator_kernel(
    nr, ng, count, slices, levels,
    part_ref, phasor_ref, expand_ref, start_ref, out_ref,
    gathered, message, sections, c_ref, x_ref, re_ref, im_ref, late_re, late_im,
    send_sem, recv_sem, send_gz, recv_gz,
):
    meet(nr, ng)
    total = share_rows(part_ref, gathered, send_sem, recv_sem, nr)
    gz = lax.axis_index("gz")
    pairs = part_ref.shape[0]
    message[:pairs] = pltpu.roll(total, gz * slices, 1)
    message[pairs:] = pltpu.roll(phasor_ref[...], gz * slices, 1)
    copies = []
    for d in range(1, ng):
        copy = pltpu.make_async_remote_copy(
            src_ref=message,
            dst_ref=sections.at[gz],
            send_sem=send_gz.at[d],
            recv_sem=recv_gz.at[d],
            device_id={"gz": lax.rem(gz + d, ng)},
            device_id_type=MESH,
        )
        copy.start()
        copies.append(copy)
    sections[gz] = message[...]
    for copy in copies:
        copy.wait()
    every = sections[0]
    for s in range(1, ng):
        every = every + sections[s]
    wide = c_ref.shape[1]
    coupled = jnp.dot(expand_ref[...], every, precision=highest, preferred_element_type=jnp.float32)
    c_ref[...] = coupled.reshape(count, wide, LANES)
    place = iota((wide, LANES), 0)
    unit = [(place == i).astype(jnp.float32) for i in range(count)]
    c = [c_ref[i] for i in range(count)]
    a = []
    for i in range(count):
        acc = unit[i]
        for k in range(count):
            acc = acc + spread(c_ref[i, pl.ds(k, 1), :], wide) * c[k]
        a.append(acc)
    for k in range(count):
        inverse = 1.0 / spread(a[k][k : k + 1], wide)
        pivot = jnp.where(place == k, inverse, a[k] * inverse)
        for i in range(count):
            if i != k:
                factor = spread(a[i][k : k + 1], wide)
                a[i] = jnp.where(place == k, 0.0, a[i]) - factor * pivot
        a[k] = pivot
    for i in range(count):
        x_ref[i] = a[i]
        re_ref[i] = 2.0 * a[i] - unit[i]
    for i in range(count):
        acc = jnp.zeros((wide, LANES), jnp.float32)
        for k in range(count):
            acc = acc + spread(x_ref[i, pl.ds(k, 1), :], wide) * c[k]
        im_ref[i] = 2.0 * acc
    lane = iota((wide, LANES), 1)

    def level(step, carry):
        shift = jnp.left_shift(1, step)
        early_re = [jnp.where(lane < shift, unit[k], pltpu.roll(re_ref[k], shift, 1)) for k in range(count)]
        early_im = [jnp.where(lane < shift, 0.0, pltpu.roll(im_ref[k], shift, 1)) for k in range(count)]
        for i in range(count):
            late_re[i] = re_ref[i]
            late_im[i] = im_ref[i]
        for i in range(count):
            new_re = jnp.zeros((wide, LANES), jnp.float32)
            new_im = jnp.zeros((wide, LANES), jnp.float32)
            for k in range(count):
                fr = spread(late_re[i, pl.ds(k, 1), :], wide)
                fi = spread(late_im[i, pl.ds(k, 1), :], wide)
                new_re = new_re + (fr * early_re[k] - fi * early_im[k])
                new_im = new_im + (fr * early_im[k] + fi * early_re[k])
            re_ref[i] = new_re
            im_ref[i] = new_im
        return carry

    lax.fori_loop(0, levels, level, 0)
    start_re = start_ref[0]
    start_im = start_ref[1]
    out_ref[...] = jnp.zeros_like(out_ref)
    for i in range(count):
        er = jnp.where(lane < 1, unit[i], pltpu.roll(re_ref[i], 1, 1))
        ei = jnp.where(lane < 1, 0.0, pltpu.roll(im_ref[i], 1, 1))
        amp_re = jnp.sum(er * start_re - ei * start_im, axis=0, keepdims=True)
        amp_im = jnp.sum(er * start_im + ei * start_re, axis=0, keepdims=True)
        out_ref[0, pl.ds(i, 1), :] = amp_re
        out_ref[1, pl.ds(i, 1), :] = amp_im


def expansion(count, wide, extra, scale):
    pairs = pair_list(count)
    rows = padded(len(pairs), 2)
    table = np.zeros((count * wide, rows + extra), np.float32)
    for index, (m, n) in enumerate(pairs):
        table[m * wide + n, index] = scale
        table[n * wide + m, index] = scale
    if extra:
        for m in range(count):
            table[m * wide + m, rows + m] = 1.0
    return table


def amplitudes(nr, ng, part, phasors, start, cells):
    slices, count = phasors.shape
    wide = padded(count, SUB)
    pairs = part.shape[0]
    expand = jnp.asarray(expansion(count, wide, wide, 2.0 / cells))
    phasor = jnp.pad(phasors.T, ((0, wide - count), (0, LANES - slices)))
    begin = jnp.broadcast_to(jnp.pad(start, ((0, 0), (0, wide - count)))[:, :, None], (2, wide, LANES))
    vmem = pl.BlockSpec(memory_space=pltpu.VMEM)
    matrix = pltpu.VMEM((count, wide, LANES), jnp.float32)
    levels = max(1, math.ceil(math.log2(slices * ng)))
    return pl.pallas_call(
        functools.partial(propagator_kernel, nr, ng, count, slices, levels),
        out_shape=jax.ShapeDtypeStruct((2, wide, LANES), jnp.float32),
        in_specs=[vmem] * 4,
        out_specs=vmem,
        scratch_shapes=[
            pltpu.VMEM((nr, pairs, LANES), jnp.float32),
            pltpu.VMEM((pairs + wide, LANES), jnp.float32),
            pltpu.VMEM((ng, pairs + wide, LANES), jnp.float32),
            matrix, matrix, matrix, matrix, matrix, matrix,
            pltpu.SemaphoreType.DMA((nr,)),
            pltpu.SemaphoreType.DMA((nr,)),
            pltpu.SemaphoreType.DMA((ng,)),
            pltpu.SemaphoreType.DMA((ng,)),
        ],
        compiler_params=pltpu.CompilerParams(collective_id=1, has_side_effects=True),
        cost_estimate=pl.CostEstimate(flops=20_000_000_000, bytes_accessed=200_000, transcendentals=0),
    )(part, phasor, expand, begin)


def final_kernel(nr, part_ref, expand_ref, out_ref, gathered, send_sem, recv_sem):
    meet(nr, 1)
    total = share_rows(part_ref, gathered, send_sem, recv_sem, nr)
    out_ref[...] = jnp.dot(expand_ref[...], total, precision=highest, preferred_element_type=jnp.float32)


def final_sums(nr, part, count, slices, cells):
    wide = padded(count, SUB)
    expand = jnp.asarray(expansion(count, wide, 0, 1.0 / cells))
    vmem = pl.BlockSpec(memory_space=pltpu.VMEM)
    out = pl.pallas_call(
        functools.partial(final_kernel, nr),
        out_shape=jax.ShapeDtypeStruct((count * wide, LANES), jnp.float32),
        in_specs=[vmem] * 2,
        out_specs=vmem,
        scratch_shapes=[
            pltpu.VMEM((nr,) + part.shape, jnp.float32),
            pltpu.SemaphoreType.DMA((nr,)),
            pltpu.SemaphoreType.DMA((nr,)),
        ],
        compiler_params=pltpu.CompilerParams(collective_id=2, has_side_effects=True),
    )(part, expand)
    return jnp.transpose(out.reshape(count, wide, LANES)[:, :count, :slices], (2, 0, 1))


def heat_kernel(
    nr,
    warm_hbm, low_hbm, high_hbm, mode_hbm, mode_low, mode_high, amp_ref,
    out_hbm, part_ref,
    natural, modes, first, second, source, pairs_ref, split_ref, total, stack_ref, lhs_ref,
    sems, out_sems,
):
    slices, rows, width = warm_hbm.shape
    count = mode_hbm.shape[0]
    halo = low_hbm.shape[1]
    tall = rows + 2 * halo
    tiles = tall // SUB
    me = lax.axis_index("rows")
    loads = [
        pltpu.make_async_copy(mode_low, modes.at[:, pl.ds(0, halo)], sems.at[0]),
        pltpu.make_async_copy(mode_hbm, modes.at[:, pl.ds(halo, rows)], sems.at[1]),
        pltpu.make_async_copy(mode_high, modes.at[:, pl.ds(halo + rows, halo)], sems.at[2]),
        pltpu.make_async_copy(low_hbm, natural.at[:, pl.ds(0, halo)], sems.at[3]),
        pltpu.make_async_copy(warm_hbm, natural.at[:, pl.ds(halo, rows)], sems.at[4]),
        pltpu.make_async_copy(high_hbm, natural.at[:, pl.ds(halo + rows, halo)], sems.at[5]),
    ]
    for load in loads:
        load.start()
    depth = stack_ref.shape[0]
    seg = count * SUB
    column = iota((amp_ref.shape[1], depth), 1)
    pick = ((column % seg) // SUB == iota((amp_ref.shape[1], depth), 0)) & (column < 3 * seg)
    wave = jnp.dot(0.1 * amp_ref[...], pick.astype(jnp.float32), precision=highest, preferred_element_type=jnp.float32)
    high = wave.astype(jnp.bfloat16).astype(jnp.float32)
    low = wave - high
    block = wave.shape[0]
    part = jnp.where(iota(wave.shape, 1) < 2 * seg, high, low)
    for r in range(SUB):
        lhs_ref[r * block : (r + 1) * block] = jnp.where(iota(wave.shape, 1) % SUB == r, part, 0.0).astype(jnp.bfloat16)
    stack_ref[...] = jnp.zeros_like(stack_ref)
    for load in loads[:3]:
        load.wait()

    def source_tile(t, carry):
        at = pl.ds(pl.multiple_of(t * SUB, SUB), SUB)
        tile = modes[:, at, :].reshape(seg, width)
        hi, lo = split(tile)
        stack_ref[:seg] = hi
        stack_ref[seg : 2 * seg] = lo
        stack_ref[2 * seg : 3 * seg] = hi
        for r in range(SUB):
            waves = jnp.dot(
                lhs_ref[r * block : (r + 1) * block], stack_ref[...], preferred_element_type=jnp.float32
            )
            re, im = waves[:slices], waves[slices:]
            source[t * SUB + r] = re * re + im * im
        return carry

    lax.fori_loop(0, tiles, source_tile, 0)
    for load in loads[3:]:
        load.wait()

    def to_rows(t, carry):
        at = pl.ds(pl.multiple_of(t * SUB, SUB), SUB)
        for c in range(0, width, LANES):
            first[at, :, c : c + LANES] = jnp.swapaxes(natural[:, at, c : c + LANES], 0, 1)
        return carry

    lax.fori_loop(0, tiles, to_rows, 0)
    second[0] = jnp.zeros_like(second[0])
    second[tall - 1] = jnp.zeros_like(second[0])
    lane = iota((1, slices, LANES), 2)
    at_first = lane == 0
    at_last = lane == LANES - 1
    bottom = jnp.where(me == 0, halo, 0)
    top = jnp.where(me == nr - 1, halo + rows, tall)

    def subcycle(src, dst, lowest, highest_row):
        group = 2

        def rows_at(g, carry):
            r = lowest + g * group
            factors = [jnp.where((r + i >= bottom) & (r + i < top), 0.2, 0.0).astype(jnp.float32) for i in range(group)]
            zero = jnp.zeros((1, slices, LANES), jnp.float32)
            columns = width // LANES

            def rolled(i, c):
                if 0 <= c < columns:
                    v = src[pl.ds(r + i, 1), :, c * LANES : (c + 1) * LANES]
                    return v, pltpu.roll(v, 1, 2), pltpu.roll(v, LANES - 1, 2)
                return zero, zero, zero

            for i in range(group):
                before = rolled(i, -1)
                here = rolled(i, 0)
                for c in range(columns):
                    after = rolled(i, c + 1)
                    lanes = slice(c * LANES, (c + 1) * LANES)
                    west = jnp.where(at_first, before[1], here[1])
                    east = jnp.where(at_last, after[2], here[2])
                    north = src[pl.ds(r + i - 1, 1), :, lanes]
                    south = src[pl.ds(r + i + 1, 1), :, lanes]
                    five = (here[0] + (north + south)) + (west + east)
                    dst[pl.ds(r + i, 1), :, lanes] = factors[i] * five + source[pl.ds(r + i, 1), :, lanes]
                    before, here = here, after
            return carry

        lax.fori_loop(0, (highest_row - lowest) // group, rows_at, 0)

    for p in range(0, PASSES, 2):
        subcycle(first, second, p + 1, tall - 1 - p)
        subcycle(second, first, p + 2, tall - 2 - p)

    total[...] = jnp.zeros_like(total)
    writes = pltpu.make_async_copy(natural.at[:, pl.ds(halo, rows)], out_hbm, out_sems.at[0])

    def from_rows(t, carry):
        at = pl.ds(pl.multiple_of(halo + t * SUB, SUB), SUB)
        for c in range(0, width, LANES):
            natural[:, at, c : c + LANES] = jnp.swapaxes(first[at, :, c : c + LANES], 0, 1)
        return carry

    lax.fori_loop(0, rows // SUB, from_rows, 0)
    writes.start()

    def sums(t, carry):
        at = pl.ds(pl.multiple_of(halo + t * SUB, SUB), SUB)
        write_pairs(count, lambda m: modes[m, at, :], pairs_ref)
        gram_step(first[at].reshape(SUB * slices, width), pairs_ref, split_ref, total)
        return carry

    lax.fori_loop(0, rows // SUB, sums, 0)
    part_ref[...] = gram_finish(total[...], slices, True)
    writes.wait()


def heat(nr, warm, low, high, modes, mode_low, mode_high, amp):
    slices, rows, width = warm.shape
    count = modes.shape[0]
    halo = low.shape[1]
    tall = rows + 2 * halo
    pair_rows = padded(len(pair_list(count)), 2) * SUB
    anywhere = pl.BlockSpec(memory_space=pltpu.HBM)
    vmem = pl.BlockSpec(memory_space=pltpu.VMEM)
    depth = padded(3 * count * SUB, LANES)
    by_row = pltpu.VMEM((tall, slices, width), jnp.float32)
    return pl.pallas_call(
        functools.partial(heat_kernel, nr),
        out_shape=(
            jax.ShapeDtypeStruct(warm.shape, jnp.float32),
            jax.ShapeDtypeStruct((pair_rows // SUB, LANES), jnp.float32),
        ),
        in_specs=[anywhere] * 6 + [vmem],
        out_specs=(anywhere, vmem),
        scratch_shapes=[
            pltpu.VMEM((slices, tall, width), jnp.float32),
            pltpu.VMEM((count, tall, width), jnp.float32),
            by_row, by_row, by_row,
            pltpu.VMEM((2 * pair_rows, width), jnp.bfloat16),
            pltpu.VMEM((2 * slices * SUB, width), jnp.bfloat16),
            pltpu.VMEM((2 * pair_rows, 2 * slices * SUB), jnp.float32),
            pltpu.VMEM((depth, width), jnp.bfloat16),
            pltpu.VMEM((SUB * 2 * slices, depth), jnp.bfloat16),
            pltpu.SemaphoreType.DMA((6,)),
            pltpu.SemaphoreType.DMA((1,)),
        ],
        compiler_params=pltpu.CompilerParams(vmem_limit_bytes=63 * MIB),
    )(warm, low, high, modes, mode_low, mode_high, amp)


def with_neighbours(block, width):
    count = lax.axis_size("rows")
    forward = [(i, i + 1) for i in range(count - 1)]
    backward = [(i + 1, i) for i in range(count - 1)]
    rows = block.shape[1]
    low = lax.ppermute(lax.slice_in_dim(block, rows - width, None, axis=1), "rows", forward)
    high = lax.ppermute(lax.slice_in_dim(block, 0, width, axis=1), "rows", backward)
    return low, high


def shards(cells, warm, modes, phasors, start):
    nr = lax.axis_size("rows")
    ng = lax.axis_size("gz")
    slices = warm.shape[0]
    count = modes.shape[0]
    mode_low, mode_high = with_neighbours(modes, PASSES)
    low, high = with_neighbours(warm, PASSES)
    part = gram(warm, modes)
    amp = amplitudes(nr, ng, part, phasors, start, cells)
    local = lax.dynamic_slice_in_dim(amp, lax.axis_index("gz") * slices, slices, axis=2)
    incoming = jnp.transpose(local, (2, 0, 1))[:, :, :count]
    by_part = jnp.transpose(local, (0, 2, 1)).reshape(2 * slices, local.shape[1])
    heated, new_part = heat(nr, warm, low, high, modes, mode_low, mode_high, by_part)
    sums = final_sums(nr, new_part, count, slices, cells)
    return heated, sums, incoming


def solution(mesh):
    placed = (P("gz", "rows", None), P(None, "rows", None), P("gz", None), P())

    def whole(warm, modes, phasors, start):
        cells = warm.shape[1] * warm.shape[2]
        return jax.shard_map(
            functools.partial(shards, cells),
            mesh=mesh,
            in_specs=placed,
            out_specs=(P("gz", "rows", None), P("gz", None, None), P("gz", None, None)),
            check_vma=False,
        )(warm, modes, phasors, start)

    return whole
```

time: 684 us -> 267 us (0.39)
  other arithmetic: 316 us -> 0 us
  Pallas kernels: 0 us -> 234 us
  matrix products: 135 us -> 0 us
  local copies, waits for them, and re-layouts: 129 us -> 16.5 us
  blocking collectives: 47.1 us -> 0 us
  starting transfers between devices: 39.6 us -> 11.2 us
  waiting for transfers between devices: 9.87 us -> 0.01 us
    pallas_call x0 -> x4, Pallas kernels: none -> 234 us  [the longest x1 195 us: heat(): pl.pallas_call(functools.partial(heat_kernel, nr), out_shape=(jax.ShapeDt...]
    add x17 -> x0, other arithmetic: 167 us -> none  [the longest x16 167 us: advance(): return center + 0.2 * laplace + 0.01 * source]
    dot_general x144 -> x0, matrix products: 135 us -> none  [the longest x2 95.1 us: slice_coupling_sums(): lax.dot_general(flat_warmth, pairs, (((1,), (1,)), ((), ())), precision=h...]
    mul x18 -> x0, other arithmetic: 131 us -> none  [the longest x16 77.4 us: shards(): widened = jnp.pad(inner, ((0, 0), (1, 1), (0, 0))) * inside]
    mul x2 -> x0, local copies, waits for them, and re-layouts: 69.1 us -> none  [pair_table(): return (flat[:, None, :] * flat[None, :, :]).reshape(count * count, -1)]
    psum x2 -> x0, blocking collectives: 47.1 us -> none  [the longest x1 24 us: shards(): beginning_value = lax.psum(partial_sums, 'rows')]
    unnamed x28 -> x15, local copies, waits for them, and re-layouts: 38.7 us -> 9.63 us
    ppermute x13 -> x4, starting transfers between devices: 39.6 us -> 11.2 us  [the longest x2 7.31 us: with_neighbours(): lax.ppermute(lax.slice_in_dim(block, 0, width, axis=1), 'rows', backward)]
  transfers between devices with their start and end apart: 13 -> 4, of which waited for: 4 -> 0; matrix products, arithmetic and copies ran while one was open for 10% -> 2% of each run, Pallas kernels for 0% -> 12%
where the time goes in v1:
time: 267 us; the launch traced here: 263 us
  Pallas kernels  234 us (88%)
  local copies, waits for them, and re-layouts  16.5 us (6%)
  starting transfers between devices  11.2 us (4%)
    pallas_call x1, Pallas kernels, heat(): pl.pallas_call(functools.partial(heat_kernel, nr), out_shape=(jax.ShapeDt...  195 us
    pallas_call x1, Pallas kernels, amplitudes(): pl.pallas_call(functools.partial(propagator_kernel, nr, ng, count, slices...  19.1 us
    pallas_call x1, Pallas kernels, gram(): pl.pallas_call(gram_kernel, grid=(rows // SUB,), out_shape=jax.ShapeDtype...  12.5 us
    unnamed x15, local copies, waits for them, and re-layouts  9.63 us
    pallas_call x1, Pallas kernels, final_sums(): pl.pallas_call(functools.partial(final_kernel, nr), out_shape=jax.ShapeDt...  7.94 us
    ppermute x2, starting transfers between devices, with_neighbours(): lax.ppermute(lax.slice_in_dim(block, 0, width, axis=1), 'rows', backward)  7.31 us
  transfers between devices with their start and end apart: 4, of which 0 were waited for; matrix products, arithmetic and copies ran while one was open for 2% of the time, Pallas kernels for 12%

profile of v1, /device:TPU:20, one launch (start us, length us, event | category | flops | bytes accessed | tf_op | source)
XLA Modules:
  0.0 262.9 jit_solution(12566595015288525000)
XLA Ops:
  0.6 2.5 fusion.1
  3.1 2.8 %collective-permute-start.3 = (f32[10,16,1024]{2,1,0:T(8,128)}, f32[10,16,1024]{2,1,0:T(8,128)S(1)}, u32[]{:S(2)}, u32[]{:S(2)}) collective-permute-start(f32[10,16,1024]{2,1,0:T(8,128)} %get-tuple-element.12), channel_id=1, source_target_pairs={{4,0},{8,4},{12,8},{16,12},{20,16},{24,20},{28,24},{5,1},{9,5},{13... | collective-permute-start | bytes 1966088 | tf_op jit(solution)/shard_map/ppermute | solution.py:491
  5.9 1.9 collective-permute-start.2
  7.8 1.7 fusion
  9.5 4.5 %collective-permute-start.1 = (f32[16,16,1024]{2,1,0:T(8,128)S(1)}, f32[16,16,1024]{2,1,0:T(8,128)}, u32[]{:S(2)}, u32[]{:S(2)}) collective-permute-start(f32[16,16,1024]{2,1,0:T(8,128)S(1)} %get-tuple-element.10), channel_id=1, source_target_pairs={{4,0},{8,4},{12,8},{16,12},{20,16},{24,20},{28,24},{5,1},{9,5},{13... | collective-permute-start | bytes 3145736 | tf_op jit(solution)/shard_map/ppermute | solution.py:491
  14.1 1.9 collective-permute-start
  16.0 0.0 copy-start
  16.0 3.4 %copy-done = f32[16,128,1024]{2,1,0:T(8,128)S(1)} copy-done((f32[16,128,1024]{2,1,0:T(8,128)S(1)}, f32[16,128,1024]{2,1,0:T(8,128)}, u32[]{:S(2)}) %copy-start) | copy-done | bytes 8388632
  19.4 0.0 copy-start.1
  19.4 2.5 copy-done.1
  21.9 0.0 copy-start.4
  21.9 0.0 copy-start.5
  21.9 12.5 %shard_map.85.part_ref = f32[56,128]{1,0:T(8,128)S(1)} custom-call(f32[16,128,1024]{2,1,0:T(8,128)S(1)} %copy-done, f32[10,128,1024]{2,1,0:T(8,128)S(1)} %copy-done.1), custom_call_target="tpu_custom_call" | custom-call | flops 20000000000 | bytes 14000000 | tf_op jit(solution)/shard_map/pallas_call | solution.py:103
  34.4 0.0 copy-start.2
  34.4 0.6 copy-done.2
  35.0 0.0 copy-done.4
  35.0 0.1 copy.9
  35.1 0.0 copy-done.5
  35.1 0.6 pad.8.phasor_ref
  35.7 0.7 broadcast_in_dim.2.start_ref
  36.4 19.1 %shard_map.86 = f32[2,16,128]{2,1,0:T(8,128)} custom-call(f32[56,128]{1,0:T(8,128)} %copy-done.2, f32[16,128]{1,0:T(8,128)} %pad.8.phasor_ref, f32[160,72]{1,0:T(8,128)} %constant.16.clone.expand_ref, f32[2,16,128]{2,1,0:T(8,128)} %broadcast_in_dim.2.start_ref), custom_call_target="tpu_custom_call" | custom-call | flops 20000000000 | bytes 200000 | tf_op jit(solution)/shard_map/pallas_call | solution.py:275
  55.5 0.8 dynamic-slice_bitcast_fusion
  56.2 0.6 copy.12
  56.9 0.7 copy.10
  57.5 0.0 collective-permute-done.3.mode_high
  57.5 0.0 copy-start.3
  57.5 0.0 collective-permute-done.2.mode_low
  57.5 0.0 collective-permute-done.1.high_hbm
  57.5 0.0 collective-permute-done.low_hbm
  57.6 0.8 copy-done.3
  58.4 195.0 %shard_map.87 = (f32[16,128,1024]{2,1,0:T(8,128)}, f32[56,128]{1,0:T(8,128)}) custom-call(f32[16,128,1024]{2,1,0:T(8,128)} %warm_hbm.1, f32[16,16,1024]{2,1,0:T(8,128)} %collective-permute-done.low_hbm, f32[16,16,1024]{2,1,0:T(8,128)} %collective-permute-done.1.high_hbm, f32[10,128,1024]{2,1,0:T(8,128)} %mode_hbm.1, ...), custom_call_target="tpu_custom_call" | custom-call | tf_op jit(solution)/shard_map/pallas_call | solution.py:461
  253.3 7.9 %shard_map.88 = f32[160,128]{1,0:T(8,128)} custom-call(f32[56,128]{1,0:T(8,128)} %get-tuple-element.6.part_ref, f32[160,56]{1,0:T(8,128)} %constant.17.clone.expand_ref), custom_call_target="tpu_custom_call" | custom-call | tf_op jit(solution)/shard_map/pallas_call | solution.py:305
  261.3 1.6 copy.13
  (1 shorter events, 0.0 us)
Async XLA Ops:
  3.1 54.4 %collective-permute-start.3 = (f32[10,16,1024]{2,1,0:T(8,128)}, f32[10,16,1024]{2,1,0:T(8,128)S(1)}, u32[]{:S(2)}, u32[]{:S(2)}) collective-permute-start(f32[10,16,1024]{2,1,0:T(8,128)} %get-tuple-element.12), channel_id=1, source_target_pairs={{4,0},{8,4},{12,8},{16,12},{20,16},{24,20},{28,24},{5,1},{9,5},{13... | collective-permute-start | bytes 1966088 | tf_op jit(solution)/shard_map/ppermute | solution.py:491
  5.9 51.6 %collective-permute-start.2 = (f32[10,16,1024]{2,1,0:T(8,128)}, f32[10,16,1024]{2,1,0:T(8,128)}, u32[]{:S(2)}, u32[]{:S(2)}) collective-permute-start(f32[10,16,1024]{2,1,0:T(8,128)} %get-tuple-element.13), channel_id=1, source_target_pairs={{0,4},{4,8},{8,12},{12,16},{16,20},{20,24},{24,28},{1,5},{5,9},{9,... | collective-permute-start | bytes 1966088 | tf_op jit(solution)/shard_map/ppermute | solution.py:490
  9.5 48.0 %collective-permute-start.1 = (f32[16,16,1024]{2,1,0:T(8,128)S(1)}, f32[16,16,1024]{2,1,0:T(8,128)}, u32[]{:S(2)}, u32[]{:S(2)}) collective-permute-start(f32[16,16,1024]{2,1,0:T(8,128)S(1)} %get-tuple-element.10), channel_id=1, source_target_pairs={{4,0},{8,4},{12,8},{16,12},{20,16},{24,20},{28,24},{5,1},{9,5},{13... | collective-permute-start | bytes 3145736 | tf_op jit(solution)/shard_map/ppermute | solution.py:491
  14.1 43.5 %collective-permute-start = (f32[16,16,1024]{2,1,0:T(8,128)S(1)}, f32[16,16,1024]{2,1,0:T(8,128)}, u32[]{:S(2)}, u32[]{:S(2)}) collective-permute-start(f32[16,16,1024]{2,1,0:T(8,128)S(1)} %get-tuple-element.11), channel_id=1, source_target_pairs={{0,4},{4,8},{8,12},{12,16},{16,20},{20,24},{24,28},{1,5},{5,9},{9,... | collective-permute-start | bytes 3145736 | tf_op jit(solution)/shard_map/ppermute | solution.py:490
  16.0 3.4 %copy-start = (f32[16,128,1024]{2,1,0:T(8,128)S(1)}, f32[16,128,1024]{2,1,0:T(8,128)}, u32[]{:S(2)}) copy-start(f32[16,128,1024]{2,1,0:T(8,128)} %warm_hbm.1) | copy-start | bytes 25165828
  19.4 2.5 copy-start.1
  21.9 13.1 %copy-start.4 = (f32[16,10]{1,0:T(8,128)S(1)}, f32[16,10]{1,0:T(8,128)}, u32[]{:S(2)}) copy-start(f32[16,10]{1,0:T(8,128)} %param.8) | copy-start | bytes 1924
  21.9 13.2 %copy-start.5 = (f32[2,10]{1,0:T(2,128)S(1)}, f32[2,10]{1,0:T(2,128)}, u32[]{:S(2)}) copy-start(f32[2,10]{1,0:T(2,128)} %param.9) | copy-start | bytes 244
  34.4 0.6 copy-start.2
  57.5 0.8 copy-start.3
